TPU v7x, 256 devices: a whole 4x4x8 slice. The times are simulated.
256 devices in a mesh: xg: 4 (over x_hi, core), yd: 64 (over x_lo, z, y).
Axes of the slice: x: 4 (x_hi: 2, x_lo: 2; x = x_hi * 2 + x_lo), y: 4, z: 8, core: 2. Of those that a mesh axis runs over, the one named last changes fastest.
Arguments:
- mobile: float32 [4096, 1, 1024], P('yd', None, 'xg'), may hold values from 0 to 2
- dispersion_x: float32 [4096, 1, 1024], P('yd', None, 'xg'), may hold values from 0.5 to 200000
- dispersion_y: float32 [4096, 1, 1024], P('yd', None, 'xg'), may hold values from 0.5 to 200000
- capacity: float32 [4096, 1, 1024], P('yd', None, 'xg'), may hold values from 0.5 to 8
- immobile: float32 [4, 4096, 1, 1024], P(None, 'yd', None, 'xg'), may hold values from 0 to 2
- exchange_rates: float32 [4], replicated, may hold values from 0.02 to 50
- rate_shares: float32 [4], replicated, may hold values from 0.1 to 1
Outputs:
- updated: float32 [4096, 1, 1024], P('yd', None, 'xg')
All inputs are finite; a program needn't handle non-finite values.
Results may differ from a plain program's by a relative error of at most 0.0003.
Values sent between devices are 32-bit elements; how exact they have to be, the bound alone decides.
A program may use at most 64 MiB of HBM per device.

v0:
```python
import jax
import jax.numpy as jnp
from jax import lax
from jax.sharding import PartitionSpec as P


def shifted_2(value, axis, steps):
    count = lax.axis_size(axis)
    pairs = [(source, (source + steps) % count) for source in range(count)]
    return lax.ppermute(value, axis, pairs)


def shifted(values, stride, axis, filling):
    length = values.shape[axis]
    if stride > 0:
        kept_part = lax.slice_in_dim(values, 0, length - stride, axis=axis)
        filler = jnp.full_like(lax.slice_in_dim(values, 0, stride, axis=axis), filling)
        return jnp.concatenate([filler, kept_part], axis=axis)
    backward = -stride
    kept_part = lax.slice_in_dim(values, backward, length, axis=axis)
    filler = jnp.full_like(lax.slice_in_dim(values, 0, backward, axis=axis), filling)
    return jnp.concatenate([kept_part, filler], axis=axis)


def pick_at(values, position, axis):
    return lax.index_in_dim(values, position, axis, keepdims=False)


def periodic_solve(face_coef, storage, right_side, axis):
    length = right_side.shape[axis]
    sub_coef = -face_coef
    super_coef = -jnp.roll(face_coef, -1, axis)
    main_coef = storage + face_coef - super_coef
    stride = 1
    while stride < length // 2:
        sub_left = jnp.roll(sub_coef, stride, axis)
        main_left = jnp.roll(main_coef, stride, axis)
        super_left = jnp.roll(super_coef, stride, axis)
        side_left = jnp.roll(right_side, stride, axis)
        sub_right = jnp.roll(sub_coef, -stride, axis)
        main_right = jnp.roll(main_coef, -stride, axis)
        super_right = jnp.roll(super_coef, -stride, axis)
        side_right = jnp.roll(right_side, -stride, axis)
        left_ratio = sub_coef / main_left
        right_ratio = super_coef / main_right
        main_coef = main_coef - left_ratio * super_left - right_ratio * sub_right
        right_side = right_side - left_ratio * side_left - right_ratio * side_right
        sub_coef = -left_ratio * sub_left
        super_coef = -right_ratio * super_right
        stride = stride * 2
    coupling = sub_coef + super_coef
    main_other = jnp.roll(main_coef, stride, axis)
    coupling_other = jnp.roll(coupling, stride, axis)
    side_other = jnp.roll(right_side, stride, axis)
    return (right_side * main_other - coupling * side_other) / (
        main_coef * main_other - coupling * coupling_other
    )


def block_solve(face_coef, storage, source, axis):
    length = source.shape[axis]
    position = lax.broadcasted_iota(jnp.int32, source.shape, axis)
    at_first = position == 0
    at_last = position == length - 1
    following = shifted(face_coef, -1, axis, 0.0)
    nothing = jnp.zeros_like(source)
    sub_coef = jnp.where(at_first | at_last, nothing, -face_coef)
    super_coef = jnp.where(at_last, nothing, -following)
    main_coef = jnp.where(at_last, 1.0, storage + face_coef + following)
    right_side = jnp.stack(
        [
            jnp.where(at_last, nothing, source),
            jnp.where(at_first, face_coef, nothing),
            jnp.where(at_last, 1.0, nothing),
        ]
    )
    stride = 1
    while stride < length:
        sub_left = shifted(sub_coef, stride, axis, 0.0)
        main_left = shifted(main_coef, stride, axis, 1.0)
        super_left = shifted(super_coef, stride, axis, 0.0)
        side_left = shifted(right_side, stride, axis + 1, 0.0)
        sub_right = shifted(sub_coef, -stride, axis, 0.0)
        main_right = shifted(main_coef, -stride, axis, 1.0)
        super_right = shifted(super_coef, -stride, axis, 0.0)
        side_right = shifted(right_side, -stride, axis + 1, 0.0)
        left_ratio = sub_coef / main_left
        right_ratio = super_coef / main_right
        right_side = right_side - left_ratio[None] * side_left - right_ratio[None] * side_right
        main_coef = main_coef - left_ratio * super_left - right_ratio * sub_right
        sub_coef = -left_ratio * sub_left
        super_coef = -right_ratio * super_right
        stride = stride * 2
    return right_side / main_coef[None]


def reduced_rows(solved, face_coef, storage, source, upcoming, axis):
    from_next, face_next = upcoming
    length = source.shape[axis]
    face_last = pick_at(face_coef, length - 1, axis)
    sub_last = -face_last
    super_last = -face_next
    main_last = pick_at(storage, length - 1, axis) + face_last + face_next
    coef_prev = sub_last * pick_at(solved[1], length - 2, axis)
    coef_self = (
        main_last + sub_last * pick_at(solved[2], length - 2, axis) + super_last * from_next[1]
    )
    coef_next = super_last * from_next[2]
    target = (
        pick_at(source, length - 1, axis)
        - sub_last * pick_at(solved[0], length - 2, axis)
        - super_last * from_next[0]
    )
    return (coef_prev, coef_self, coef_next, target)


def dense_cyclic(all_rows, group_size):
    matrix_rows = []
    targets = []
    for row_index in range(group_size):
        entries = [jnp.zeros_like(all_rows[row_index, 1]) for column in range(group_size)]
        entries[(row_index - 1) % group_size] = all_rows[row_index, 0]
        entries[row_index] = all_rows[row_index, 1]
        entries[(row_index + 1) % group_size] = all_rows[row_index, 2]
        matrix_rows.append(entries)
        targets.append(all_rows[row_index, 3])
    for pivot in range(group_size):
        for row_index in range(pivot + 1, group_size):
            factor = matrix_rows[row_index][pivot] / matrix_rows[pivot][pivot]
            matrix_rows[row_index] = [
                matrix_rows[row_index][column] - factor * matrix_rows[pivot][column]
                for column in range(group_size)
            ]
            targets[row_index] = targets[row_index] - factor * targets[pivot]
    solutions = [None] * group_size
    for row_index in reversed(range(group_size)):
        total = targets[row_index]
        for column in range(row_index + 1, group_size):
            total = total - matrix_rows[row_index][column] * solutions[column]
        solutions[row_index] = total / matrix_rows[row_index][row_index]
    return jnp.stack(solutions)


def local(mobile, dispersion_x, dispersion_y, capacity, immobile, exchange_rates, rate_shares):
    weights = rate_shares * exchange_rates / (1.0 + exchange_rates)
    gain_terms = capacity[None] * weights[:, None, None, None]
    storage = 1.0 + jnp.sum(gain_terms, axis=0)
    source = mobile + jnp.sum(gain_terms * immobile, axis=0)
    solved = block_solve(dispersion_x, storage, source, 2)
    head_values = pick_at(solved, 0, 3)
    upcoming = shifted_2((head_values, pick_at(dispersion_x, 0, 2)), "xg", -1)
    rows = reduced_rows(solved, dispersion_x, storage, source, upcoming, 2)
    group_size = lax.axis_size("xg")
    all_rows = lax.all_gather(jnp.stack(rows)[None], "xg", axis=0, tiled=True)
    solutions = dense_cyclic(all_rows, group_size)
    own_index = lax.axis_index("xg")
    own_value = lax.dynamic_index_in_dim(solutions, own_index, 0, keepdims=False)
    prev_value = lax.dynamic_index_in_dim(
        solutions, (own_index + group_size - 1) % group_size, 0, keepdims=False
    )
    after_x = solved[0] + solved[1] * prev_value[..., None] + solved[2] * own_value[..., None]
    group_count = lax.axis_size("yd")

    def regroup(values):
        return values.reshape(values.shape[0], group_count, -1)

    line_values = lax.all_to_all(regroup(after_x), "yd", split_axis=1, concat_axis=0, tiled=True)
    line_faces = lax.all_to_all(
        regroup(dispersion_y), "yd", split_axis=1, concat_axis=0, tiled=True
    )
    line_storage = lax.all_to_all(regroup(storage), "yd", split_axis=1, concat_axis=0, tiled=True)
    solved_lines = periodic_solve(line_faces, line_storage, line_storage * line_values, 0)
    updated = lax.all_to_all(solved_lines, "yd", split_axis=0, concat_axis=1, tiled=True)
    updated = updated.reshape(after_x.shape)
    return updated


def solution(mesh):
    return jax.shard_map(
        local,
        mesh=mesh,
        in_specs=(
            P("yd", None, "xg"),
            P("yd", None, "xg"),
            P("yd", None, "xg"),
            P("yd", None, "xg"),
            P(None, "yd", None, "xg"),
            P(),
            P(),
        ),
        out_specs=P("yd", None, "xg"),
        check_vma=False,
    )
```

profile of v0, /device:TPU:4, one launch (start us, length us, event | category | flops | bytes accessed | tf_op | source)
XLA Modules:
  0.0 107.0 jit_solution(12925277914980473333)
XLA Ops:
  0.0 0.8 copy.95
  0.9 0.8 copy.55
  2.5 1.6 %fusion = (f32[64,256]{1,0:T(8,128)S(1)}, f32[64,256]{1,0:T(8,128)S(1)}) fusion(f32[4,64,1,256]{3,2,1,0:T(1,128)} %param.11, f32[64,256]{1,0:T(8,128)S(1)} %bitcast.400, f32[4]{0:T(128)S(1)} %add_divide_fusion), kind=kLoop, calls=%fused_computation.2 | loop fusion | flops 229376 | bytes 458768 | tf_op jit(solution)/shard_map/reduce_sum | solution.py:148
  4.1 0.9 add_select_fusion
  5.1 0.9 fusion.90
  12.3 2.4 %collective-permute-start = (f32[64,1]{0,1:T(1,128)S(1)}, f32[64,1]{0,1:T(1,128)S(1)}, u32[]{:S(2)}, u32[]{:S(2)}) collective-permute-start(f32[64,1]{0,1:T(1,128)S(1)} %bitcast.403), channel_id=1, source_target_pairs={{0,192},{64,0},{128,64},{192,128},{1,193},{65,1},{129,65},{193,129... | collective-permute-start | bytes 776 | tf_op jit(solution)/shard_map/ppermute | solution.py:10
  14.8 0.8 reshape.21111
  15.6 11.9 %all-to-all-start.2 = ((f32[64,1,256]{2,1,0:T(1,128)}), f32[64,1,256]{2,1,0:T(1,128)S(1)}, u32[]{:S(2)}, u32[]{:S(2)}) async-start(f32[64,1,256]{2,1,0:T(1,128)} %reshape.21111), calls=%async_computation.2 | async-start | bytes 131072 | tf_op jit(solution)/shard_map/all_to_all | solution.py:168
  28.2 0.8 reshape.21113
  29.0 6.7 %all-gather = f32[16,64,1]{1,2,0:T(1,128)S(1)} all-gather(f32[4,64,1]{1,2,0:T(1,128)S(1)} %pad_maximum_fusion.2), channel_id=2, replica_groups=mesh['xg'=4,'yd'=64] {'xg'}, dimensions={0}, use_global_device_ids=true | all-gather | bytes 5120 | tf_op jit(solution)/shard_map/all_gather | solution.py:154
  35.9 0.8 reshape.21115
  36.6 1.7 %all-to-all-done.2 = f32[64,1,256]{2,1,0:T(1,128)S(1)} async-done(((f32[64,1,256]{2,1,0:T(1,128)}), f32[64,1,256]{2,1,0:T(1,128)S(1)}, u32[]{:S(2)}, u32[]{:S(2)}) %all-to-all-start.2) | async-done | bytes 65568 | tf_op jit(solution)/shard_map/all_to_all | solution.py:168
  38.3 9.6 %all-to-all-start = ((f32[64,1,256]{2,1,0:T(1,128)}), f32[64,1,256]{2,1,0:T(1,128)S(1)}, u32[]{:S(2)}, u32[]{:S(2)}) async-start(f32[64,1,256]{2,1,0:T(1,128)} %reshape.21113), calls=%async_computation | async-start | bytes 131072 | tf_op jit(solution)/shard_map/all_to_all | solution.py:171
  48.5 0.8 reduce.15
  49.6 9.1 %all-to-all-done = f32[64,1,256]{2,1,0:T(1,128)S(1)} async-done(((f32[64,1,256]{2,1,0:T(1,128)}), f32[64,1,256]{2,1,0:T(1,128)S(1)}, u32[]{:S(2)}, u32[]{:S(2)}) %all-to-all-start) | async-done | bytes 65568 | tf_op jit(solution)/shard_map/all_to_all | solution.py:171
  58.7 4.8 %all-to-all-start.1 = ((f32[64,1,256]{2,1,0:T(1,128)}), f32[64,1,256]{2,1,0:T(1,128)S(1)}, u32[]{:S(2)}, u32[]{:S(2)}) async-start(f32[64,1,256]{2,1,0:T(1,128)} %reshape.21115), calls=%async_computation.1 | async-start | bytes 131072 | tf_op jit(solution)/shard_map/all_to_all | solution.py:167
  63.5 0.8 reduce.14
  64.5 9.5 %all-to-all-done.1 = f32[64,1,256]{2,1,0:T(1,128)S(1)} async-done(((f32[64,1,256]{2,1,0:T(1,128)}), f32[64,1,256]{2,1,0:T(1,128)S(1)}, u32[]{:S(2)}, u32[]{:S(2)}) %all-to-all-start.1) | async-done | bytes 65568 | tf_op jit(solution)/shard_map/all_to_all | solution.py:167
  74.1 0.8 reduce.16
  85.0 1.7 %reshape.21117 = f32[64,1,256]{2,1,0:T(1,128)S(1)} reshape(f32[4096,4]{1,0:T(8,128)S(1)} %copy.96) | data formatting | bytes 131072
  86.7 14.6 %all_to_all.69 = f32[64,1,256]{2,1,0:T(1,128)S(1)} all-to-all(f32[64,1,256]{2,1,0:T(1,128)S(1)} %reshape.21117), channel_id=1, replica_groups=mesh['xg'=4,'yd'=64] {'yd'}, dimensions={0} | all-to-all | bytes 131072 | tf_op jit(solution)/shard_map/all_to_all | solution.py:173
  101.3 0.8 reduce.18
  102.1 3.4 %reshape.21118 = f32[4096,1,4]{2,1,0:T(1,128)S(1)} reshape(f32[64,256]{1,0:T(8,128)S(1)} %reduce.18) | data formatting | bytes 131072
  106.3 0.7 copy.85
  (228 shorter events, 19.2 us)
Async XLA Ops:
  0.0 6.0 %copy-start = (f32[64,1,256]{2,1,0:T(1,128)S(1)}, f32[64,1,256]{2,1,0:T(1,128)}, u32[]{:S(2)}) copy-start(f32[64,1,256]{2,1,0:T(1,128)} %param.8) | copy-start | bytes 196612
  11.1 3.6 %copy-start.1 = (f32[64,1,256]{2,1,0:T(1,128)S(1)}, f32[64,1,256]{2,1,0:T(1,128)}, u32[]{:S(2)}) copy-start(f32[64,1,256]{2,1,0:T(1,128)} %param.9) | copy-start | bytes 196612
  11.7 17.3 %collective-permute-start.1 = (f32[3,64,1]{1,2,0:T(1,128)S(1)}, f32[3,64,1]{1,2,0:T(1,128)S(1)}, u32[]{:S(2)}, u32[]{:S(2)}) collective-permute-start(f32[3,64,1]{1,2,0:T(1,128)S(1)} %squeeze.95), channel_id=1, source_target_pairs={{0,192},{64,0},{128,64},{192,128},{1,193},{65,1},{129,65},{193,129... | collective-permute-start | bytes 2312 | tf_op jit(solution)/shard_map/ppermute | solution.py:10
  12.3 16.7 %collective-permute-start = (f32[64,1]{0,1:T(1,128)S(1)}, f32[64,1]{0,1:T(1,128)S(1)}, u32[]{:S(2)}, u32[]{:S(2)}) collective-permute-start(f32[64,1]{0,1:T(1,128)S(1)} %bitcast.403), channel_id=1, source_target_pairs={{0,192},{64,0},{128,64},{192,128},{1,193},{65,1},{129,65},{193,129... | collective-permute-start | bytes 776 | tf_op jit(solution)/shard_map/ppermute | solution.py:10
  15.6 22.7 %all-to-all-start.2 = ((f32[64,1,256]{2,1,0:T(1,128)}), f32[64,1,256]{2,1,0:T(1,128)S(1)}, u32[]{:S(2)}, u32[]{:S(2)}) async-start(f32[64,1,256]{2,1,0:T(1,128)} %reshape.21111), calls=%async_computation.2 | async-start | bytes 131072 | tf_op jit(solution)/shard_map/all_to_all | solution.py:168
  38.3 20.4 %all-to-all-start = ((f32[64,1,256]{2,1,0:T(1,128)}), f32[64,1,256]{2,1,0:T(1,128)S(1)}, u32[]{:S(2)}, u32[]{:S(2)}) async-start(f32[64,1,256]{2,1,0:T(1,128)} %reshape.21113), calls=%async_computation | async-start | bytes 131072 | tf_op jit(solution)/shard_map/all_to_all | solution.py:171
  58.7 15.4 %all-to-all-start.1 = ((f32[64,1,256]{2,1,0:T(1,128)}), f32[64,1,256]{2,1,0:T(1,128)S(1)}, u32[]{:S(2)}, u32[]{:S(2)}) async-start(f32[64,1,256]{2,1,0:T(1,128)} %reshape.21115), calls=%async_computation.1 | async-start | bytes 131072 | tf_op jit(solution)/shard_map/all_to_all | solution.py:167
where the time goes:
time: 108 us; the launch traced here: 107 us
  starting transfers between devices  28.8 us (27%)
  local copies, waits for them, and re-layouts  21.3 us (20%)
  blocking collectives  21.3 us (20%)
  waiting for transfers between devices  20.3 us (19%)
  other arithmetic  14.1 us (13%)
  between operations  1.29 us (1%)
    all_to_all x1, blocking collectives, local(): lax.all_to_all(solved_lines, 'yd', split_axis=0, concat_axis=1, tiled=True)  14.6 us
    all_to_all x1, starting transfers between devices, local(): lax.all_to_all(regroup(dispersion_y), 'yd', split_axis=1, concat_axis=0,...  11.9 us
    unnamed x16, local copies, waits for them, and re-layouts  10.2 us
    all_to_all x1, starting transfers between devices, local(): lax.all_to_all(regroup(storage), 'yd', split_axis=1, concat_axis=0, tiled...  9.63 us
    all_to_all x1, waiting for transfers between devices, local(): lax.all_to_all(regroup(after_x), 'yd', split_axis=1, concat_axis=0, tiled...  9.53 us
    all_to_all x1, waiting for transfers between devices, local(): lax.all_to_all(regroup(storage), 'yd', split_axis=1, concat_axis=0, tiled...  9.06 us
    all_gather x1, blocking collectives, local(): all_rows = lax.all_gather(jnp.stack(rows)[None], 'xg', axis=0, tiled=True)  6.7 us
    all_to_all x1, starting transfers between devices, local(): lax.all_to_all(regroup(after_x), 'yd', split_axis=1, concat_axis=0, tiled...  4.8 us
  transfers between devices with their start and end apart: 5, of which 3 were waited for; matrix products, arithmetic and copies ran while one was open for 6% of the time, Pallas kernels for 0%

commit v1 on v0

--- a/solution.py
+++ b/solution.py
@@ -1,7 +1,20 @@
+import functools
 import jax
 import jax.numpy as jnp
 from jax import lax
 from jax.sharding import PartitionSpec as P
+
+
+def recast_view(base_x, link_axis, dim_k):
+    sides = []
+    for _ in range(lax.axis_size(link_axis)):
+        sides.append(base_x)
+    view_out = jnp.stack(sides)
+    part_now = lax.all_to_all(view_out, axis_name=link_axis, split_axis=0, concat_axis=0)
+    return jnp.concatenate(part_now, dim_k)
+
+
+place_things = functools.partial(recast_view, link_axis="xg", dim_k=0)
 
 
 def shifted_2(value, axis, steps):
@@ -151,7 +164,7 @@
     upcoming = shifted_2((head_values, pick_at(dispersion_x, 0, 2)), "xg", -1)
     rows = reduced_rows(solved, dispersion_x, storage, source, upcoming, 2)
     group_size = lax.axis_size("xg")
-    all_rows = lax.all_gather(jnp.stack(rows)[None], "xg", axis=0, tiled=True)
+    all_rows = place_things(jnp.stack(rows)[None])
     solutions = dense_cyclic(all_rows, group_size)
     own_index = lax.axis_index("xg")
     own_value = lax.dynamic_index_in_dim(solutions, own_index, 0, keepdims=False)

time: 108 us -> 114 us (1.056); the launches traced: 107 us -> 112 us
  waiting for transfers between devices: 20.3 us -> 28.6 us
  blocking collectives: 21.3 us -> 14.6 us
  starting transfers between devices: 28.8 us -> 30.3 us
    all_to_all x1, waiting for transfers between devices: 1.66 us -> 8.5 us  [local(): lax.all_to_all(regroup(dispersion_y), 'yd', split_axis=1, concat_axis=0,...]
    all_gather x1 -> x0, blocking collectives: 6.7 us -> none  [local(): all_rows = lax.all_gather(jnp.stack(rows)[None], 'xg', axis=0, tiled=True)]
    all_to_all x0 -> x1, starting transfers between devices: none -> 5.8 us  [recast_view(): lax.all_to_all(view_out, axis_name=link_axis, split_axis=0, concat_axis=0)]
    all_to_all x1, starting transfers between devices: 9.63 us -> 4.62 us  [local(): lax.all_to_all(regroup(storage), 'yd', split_axis=1, concat_axis=0, tiled...]
    unnamed x16 -> x19, local copies, waits for them, and re-layouts: 10.2 us -> 10.9 us
  transfers between devices with their start and end apart: 5 -> 6, of which waited for: 3 -> 4; matrix products, arithmetic and copies ran while one was open for 6% -> 6% of each run, Pallas kernels for 0% -> 0%
where the time goes in v1:
time: 114 us; the launch traced here: 112 us
  starting transfers between devices  30.3 us (27%)
  waiting for transfers between devices  28.6 us (25%)
  local copies, waits for them, and re-layouts  22.1 us (19%)
  other arithmetic  15.1 us (13%)
  blocking collectives  14.6 us (13%)
  between operations  1.27 us (1%)
    all_to_all x1, blocking collectives, local(): lax.all_to_all(solved_lines, 'yd', split_axis=0, concat_axis=1, tiled=True)  14.6 us
    all_to_all x1, starting transfers between devices, local(): lax.all_to_all(regroup(dispersion_y), 'yd', split_axis=1, concat_axis=0,...  12.7 us
    unnamed x19, local copies, waits for them, and re-layouts  10.9 us
    all_to_all x1, waiting for transfers between devices, local(): lax.all_to_all(regroup(storage), 'yd', split_axis=1, concat_axis=0, tiled...  9.57 us
    all_to_all x1, waiting for transfers between devices, local(): lax.all_to_all(regroup(after_x), 'yd', split_axis=1, concat_axis=0, tiled...  9.5 us
    all_to_all x1, waiting for transfers between devices, local(): lax.all_to_all(regroup(dispersion_y), 'yd', split_axis=1, concat_axis=0,...  8.5 us
    all_to_all x1, starting transfers between devices, recast_view(): lax.all_to_all(view_out, axis_name=link_axis, split_axis=0, concat_axis=0)  5.8 us
    all_to_all x1, starting transfers between devices, local(): lax.all_to_all(regroup(after_x), 'yd', split_axis=1, concat_axis=0, tiled...  4.73 us
  transfers between devices with their start and end apart: 6, of which 4 were waited for; matrix products, arithmetic and copies ran while one was open for 6% of the time, Pallas kernels for 0%

profile of v1, /device:TPU:4, one launch (start us, length us, event | category | flops | bytes accessed | tf_op | source)
XLA Modules:
  0.0 111.9 jit_solution(11693296545759484907)
XLA Ops:
  0.0 0.8 copy.47
  0.9 0.8 copy.23
  2.5 1.6 %fusion = (f32[64,256]{1,0:T(8,128)S(1)}, f32[64,256]{1,0:T(8,128)S(1)}) fusion(f32[4,64,1,256]{3,2,1,0:T(1,128)} %param.11, f32[64,256]{1,0:T(8,128)S(1)} %bitcast.404, f32[4]{0:T(128)S(1)} %add_divide_fusion), kind=kLoop, calls=%fused_computation.2 | loop fusion | flops 229376 | bytes 458768 | tf_op jit(solution)/shard_map/reduce_sum | solution.py:161
  4.1 0.9 add_select_fusion
  5.1 0.9 fusion.90
  12.3 2.4 %collective-permute-start = (f32[64,1]{0,1:T(1,128)S(1)}, f32[64,1]{0,1:T(1,128)S(1)}, u32[]{:S(2)}, u32[]{:S(2)}) collective-permute-start(f32[64,1]{0,1:T(1,128)S(1)} %bitcast.407), channel_id=1, source_target_pairs={{0,192},{64,0},{128,64},{192,128},{1,193},{65,1},{129,65},{193,129... | collective-permute-start | bytes 776 | tf_op jit(solution)/shard_map/ppermute | solution.py:23
  15.0 1.0 collective-permute-done
  16.7 5.8 %all-to-all-start.1 = ((f32[4,1,256]{2,1,0:T(1,128)}), f32[4,1,256]{2,1,0:T(1,128)S(1)}, u32[]{:S(2)}, u32[]{:S(2)}) async-start(f32[4,1,256]{2,1,0:T(1,128)} %reshape.21121), calls=%async_computation.1 | async-start | bytes 8192 | tf_op jit(solution)/shard_map/all_to_all | solution.py:13
  22.9 0.8 reshape.21119
  23.8 0.8 reshape.21117
  24.6 12.7 %all-to-all-start.3 = ((f32[64,1,256]{2,1,0:T(1,128)}), f32[64,1,256]{2,1,0:T(1,128)S(1)}, u32[]{:S(2)}, u32[]{:S(2)}) async-start(f32[64,1,256]{2,1,0:T(1,128)} %reshape.21117), calls=%async_computation.3 | async-start | bytes 131072 | tf_op jit(solution)/shard_map/all_to_all | solution.py:181
  38.8 0.8 reshape.21123
  39.6 8.5 %all-to-all-done.3 = f32[64,1,256]{2,1,0:T(1,128)S(1)} async-done(((f32[64,1,256]{2,1,0:T(1,128)}), f32[64,1,256]{2,1,0:T(1,128)S(1)}, u32[]{:S(2)}, u32[]{:S(2)}) %all-to-all-start.3) | async-done | bytes 65568 | tf_op jit(solution)/shard_map/all_to_all | solution.py:181
  48.1 4.6 %all-to-all-start = ((f32[64,1,256]{2,1,0:T(1,128)}), f32[64,1,256]{2,1,0:T(1,128)S(1)}, u32[]{:S(2)}, u32[]{:S(2)}) async-start(f32[64,1,256]{2,1,0:T(1,128)} %reshape.21119), calls=%async_computation | async-start | bytes 131072 | tf_op jit(solution)/shard_map/all_to_all | solution.py:184
  52.7 0.8 reduce.15
  53.9 9.6 %all-to-all-done = f32[64,1,256]{2,1,0:T(1,128)S(1)} async-done(((f32[64,1,256]{2,1,0:T(1,128)}), f32[64,1,256]{2,1,0:T(1,128)S(1)}, u32[]{:S(2)}, u32[]{:S(2)}) %all-to-all-start) | async-done | bytes 65568 | tf_op jit(solution)/shard_map/all_to_all | solution.py:184
  63.5 4.7 %all-to-all-start.2 = ((f32[64,1,256]{2,1,0:T(1,128)}), f32[64,1,256]{2,1,0:T(1,128)S(1)}, u32[]{:S(2)}, u32[]{:S(2)}) async-start(f32[64,1,256]{2,1,0:T(1,128)} %reshape.21123), calls=%async_computation.2 | async-start | bytes 131072 | tf_op jit(solution)/shard_map/all_to_all | solution.py:180
  68.2 0.8 reduce.14
  69.3 9.5 %all-to-all-done.2 = f32[64,1,256]{2,1,0:T(1,128)S(1)} async-done(((f32[64,1,256]{2,1,0:T(1,128)}), f32[64,1,256]{2,1,0:T(1,128)S(1)}, u32[]{:S(2)}, u32[]{:S(2)}) %all-to-all-start.2) | async-done | bytes 65568 | tf_op jit(solution)/shard_map/all_to_all | solution.py:180
  78.8 0.8 reduce.17
  89.8 1.7 %reshape.21125 = f32[64,1,256]{2,1,0:T(1,128)S(1)} reshape(f32[4096,4]{1,0:T(8,128)S(1)} %copy.48) | data formatting | bytes 131072
  91.6 14.6 %all_to_all.74 = f32[64,1,256]{2,1,0:T(1,128)S(1)} all-to-all(f32[64,1,256]{2,1,0:T(1,128)S(1)} %reshape.21125), channel_id=1, replica_groups=mesh['xg'=4,'yd'=64] {'yd'}, dimensions={0} | all-to-all | bytes 131072 | tf_op jit(solution)/shard_map/all_to_all | solution.py:186
  106.1 0.8 reduce.19
  107.0 3.4 %reshape.21126 = f32[4096,1,4]{2,1,0:T(1,128)S(1)} reshape(f32[64,256]{1,0:T(8,128)S(1)} %reduce.19) | data formatting | bytes 131072
  (234 shorter events, 21.5 us)
Async XLA Ops:
  0.0 6.0 %copy-start = (f32[64,1,256]{2,1,0:T(1,128)S(1)}, f32[64,1,256]{2,1,0:T(1,128)}, u32[]{:S(2)}) copy-start(f32[64,1,256]{2,1,0:T(1,128)} %param.8) | copy-start | bytes 196612
  11.5 12.2 %copy-start.1 = (f32[64,1,256]{2,1,0:T(1,128)S(1)}, f32[64,1,256]{2,1,0:T(1,128)}, u32[]{:S(2)}) copy-start(f32[64,1,256]{2,1,0:T(1,128)} %param.9) | copy-start | bytes 196612
  11.7 4.3 %collective-permute-start.1 = (f32[3,64,1]{1,2,0:T(1,128)S(1)}, f32[3,64,1]{1,2,0:T(1,128)S(1)}, u32[]{:S(2)}, u32[]{:S(2)}) collective-permute-start(f32[3,64,1]{1,2,0:T(1,128)S(1)} %squeeze.95), channel_id=1, source_target_pairs={{0,192},{64,0},{128,64},{192,128},{1,193},{65,1},{129,65},{193,129... | collective-permute-start | bytes 2312 | tf_op jit(solution)/shard_map/ppermute | solution.py:23
  12.3 3.7 %collective-permute-start = (f32[64,1]{0,1:T(1,128)S(1)}, f32[64,1]{0,1:T(1,128)S(1)}, u32[]{:S(2)}, u32[]{:S(2)}) collective-permute-start(f32[64,1]{0,1:T(1,128)S(1)} %bitcast.407), channel_id=1, source_target_pairs={{0,192},{64,0},{128,64},{192,128},{1,193},{65,1},{129,65},{193,129... | collective-permute-start | bytes 776 | tf_op jit(solution)/shard_map/ppermute | solution.py:23
  16.7 7.9 %all-to-all-start.1 = ((f32[4,1,256]{2,1,0:T(1,128)}), f32[4,1,256]{2,1,0:T(1,128)S(1)}, u32[]{:S(2)}, u32[]{:S(2)}) async-start(f32[4,1,256]{2,1,0:T(1,128)} %reshape.21121), calls=%async_computation.1 | async-start | bytes 8192 | tf_op jit(solution)/shard_map/all_to_all | solution.py:13
  24.6 23.5 %all-to-all-start.3 = ((f32[64,1,256]{2,1,0:T(1,128)}), f32[64,1,256]{2,1,0:T(1,128)S(1)}, u32[]{:S(2)}, u32[]{:S(2)}) async-start(f32[64,1,256]{2,1,0:T(1,128)} %reshape.21117), calls=%async_computation.3 | async-start | bytes 131072 | tf_op jit(solution)/shard_map/all_to_all | solution.py:181
  48.1 15.4 %all-to-all-start = ((f32[64,1,256]{2,1,0:T(1,128)}), f32[64,1,256]{2,1,0:T(1,128)S(1)}, u32[]{:S(2)}, u32[]{:S(2)}) async-start(f32[64,1,256]{2,1,0:T(1,128)} %reshape.21119), calls=%async_computation | async-start | bytes 131072 | tf_op jit(solution)/shard_map/all_to_all | solution.py:184
  63.5 15.3 %all-to-all-start.2 = ((f32[64,1,256]{2,1,0:T(1,128)}), f32[64,1,256]{2,1,0:T(1,128)S(1)}, u32[]{:S(2)}, u32[]{:S(2)}) async-start(f32[64,1,256]{2,1,0:T(1,128)} %reshape.21123), calls=%async_computation.2 | async-start | bytes 131072 | tf_op jit(solution)/shard_map/all_to_all | solution.py:180
